TPU v7x, 32 devices: a whole 2x2x4 slice. The times are simulated.
32 devices in a mesh: ens: 2 (over x), tile: 16 (over z, y, core).
Axes of the slice: x: 2, y: 2, z: 4, core: 2. Of those that a mesh axis runs over, the one named last changes fastest.
Arguments:
- final_adjoint: float32 [320, 32, 1024], P('ens', 'tile'), parts along dimension 0, may hold values from -0.5 to 1.5
- first_density: float32 [320, 32, 1024], P('ens', 'tile'), parts along dimension 0, may hold values from 0.05 to 2
- second_density: float32 [320, 32, 1024], P('ens', 'tile'), parts along dimension 0, may hold values from 0.05 to 2
- forage: float32 [4, 6, 32, 1024], P('ens', None, 'tile'), parts along dimension 0, may hold values from 5 to 50
- preference: float32 [32, 6], P('ens'), parts along dimension 0, may hold values from 0.02 to 0.3
- base_mortality: float32 [160], replicated, may hold values from 0.01 to 0.5
- age_class: int32 [160], replicated, may hold values from 0 to 15, never falling along the last dimension, each value on 1 to 20 neighbouring positions
- land_mask: int32 [32, 1024], P('tile'), may hold values 0 or 1
- east_velocity: float32 [32, 1024], P('tile'), may hold values from -0.1 to 0.1
- north_velocity: float32 [32, 1024], P('tile'), may hold values from -0.1 to 0.1
Outputs:
- initial_adjoint: float32 [320, 32, 1024], P('ens', 'tile'), parts along dimension 0
- forage_sensitivity: float32 [4, 6, 32, 1024], P('ens', None, 'tile'), parts along dimension 0
- preference_gradient: float32 [32, 6], P('ens'), parts along dimension 0
There are 2 independent parts, one for each index of `ens`. A program takes and returns all parts, laid end to end along the dimension named above; an argument that names none is the same for every part. Nothing has to cross between parts.
Inputs may be any that keep to these rules, and one draw needn't show every extreme that they name: `age_class`: never falls along the cohorts; every class holds 1 to 20 cohorts, one exactly that many.
All inputs are finite; a program needn't handle non-finite values. No bound on the sum of `land_mask` on one device may be relied on, other than what follows from the above.
Results may differ from a plain program's by a relative error of at most 0.00011.
Values sent between devices are 32-bit elements; how exact they have to be, the bound alone decides.
A program may use at most 64 MiB of HBM per device.

v0:
```python
import jax
import jax.numpy as jnp
from jax import lax
from jax.sharding import PartitionSpec as P

SUBSTEPS = 4
HIGH = lax.Precision.HIGHEST


def with_halo(cells, sides, width):
    for axis, dim in sides:
        count = lax.axis_size(axis)
        ends = count - 1
        head = lax.slice_in_dim(cells, 0, width, axis=dim)
        tail = lax.slice_in_dim(cells, cells.shape[dim] - width, cells.shape[dim], axis=dim)
        cells = jnp.concatenate(
            [
                lax.ppermute(tail, axis, [(i, (i + 1) % count) for i in range(ends)]),
                cells,
                lax.ppermute(head, axis, [((i + 1) % count, i) for i in range(ends)]),
            ],
            axis=dim,
        )
    return cells


def make_rates(extended):
    mask = extended[0]
    centre = mask[1:-1]
    east_velocity = extended[1][1:-1]
    north_velocity = extended[2][1:-1]
    rate_n = centre * mask[:-2] * (0.1 + jnp.maximum(north_velocity, 0.0))
    rate_s = centre * mask[2:] * (0.1 + jnp.maximum(-north_velocity, 0.0))
    rate_e = centre * jnp.roll(centre, -1, axis=1) * (0.1 + jnp.maximum(east_velocity, 0.0))
    rate_w = centre * jnp.roll(centre, 1, axis=1) * (0.1 + jnp.maximum(-east_velocity, 0.0))
    keep = 1.0 - rate_n - rate_s - rate_e - rate_w
    return (keep, rate_n, rate_s, rate_e, rate_w)


def transpose_step(padded, first_row, rates):
    count = padded.shape[1] - 2
    begin = first_row + 1
    keep, rate_n, rate_s, rate_e, rate_w = [r[begin : begin + count] for r in rates]
    centre = padded[:, 1:-1]
    return (
        keep * centre
        + rate_n * padded[:, :-2]
        + rate_s * padded[:, 2:]
        + rate_e * jnp.roll(centre, -1, axis=2)
        + rate_w * jnp.roll(centre, 1, axis=2)
    )


def transported(incoming, rates):
    carried = incoming

    def one_step(index, field):
        wide = with_halo(field, (("tile", 1),), 1)
        return transpose_step(wide, 0, rates)

    carried = lax.fori_loop(0, SUBSTEPS, one_step, carried)
    return carried


def month_adjoint(incoming, density, food, pref_rows, base_mortality, rates, onehot):
    carried = transported(incoming, rates)
    cohorts = carried.shape[0]
    aged = jnp.concatenate([carried[1:], carried[cohorts - 1 :]], axis=0).reshape(cohorts, -1)
    dens = density.reshape(cohorts, -1)
    feed = food.reshape(food.shape[0], -1)
    demand = jnp.dot(pref_rows.T, dens, precision=HIGH)
    total = feed + demand
    short = demand / total
    survival = jnp.exp(-(base_mortality[:, None] + jnp.dot(pref_rows, short, precision=HIGH)))
    grown = survival * dens
    adj_mort = -aged * grown
    adj_ratio = -jnp.dot(pref_rows.T, adj_mort, precision=HIGH)
    squared = total * total
    adj_demand = -adj_ratio * feed / squared
    sensitivity = adj_ratio * demand * feed / squared
    outgoing = aged * survival + jnp.dot(pref_rows, adj_demand, precision=HIGH)
    cohort_grad = jnp.dot(adj_mort, short.T, precision=HIGH) + jnp.dot(
        dens, adj_demand.T, precision=HIGH
    )
    class_grad = jnp.dot(onehot, cohort_grad, precision=HIGH)
    return (outgoing.reshape(density.shape), sensitivity.reshape(food.shape), class_grad)


def shards(
    final_adjoint,
    first_density,
    second_density,
    forage,
    preference,
    base_mortality,
    age_class,
    land_mask,
    east_velocity,
    north_velocity,
):
    classes = preference.shape[0]
    onehot = (age_class[None, :] == jnp.arange(classes, dtype=jnp.int32)[:, None]).astype(
        jnp.float32
    )
    pref_rows = jnp.dot(onehot.T, preference, precision=HIGH)
    fields = jnp.stack([land_mask.astype(jnp.float32), east_velocity, north_velocity], axis=0)
    extended = with_halo(fields, (("tile", 1),), 2)
    rates = make_rates(extended)
    cells = land_mask.shape[0] * lax.axis_size("tile") * land_mask.shape[1]
    middle, sens_two, grad_two = month_adjoint(
        final_adjoint, second_density, forage[1], pref_rows, base_mortality, rates, onehot
    )

    def month_total(local_grad):
        return lax.psum(local_grad, "tile")

    total_two = month_total(grad_two)
    initial, sens_one, grad_one = month_adjoint(
        middle, first_density, forage[0], pref_rows, base_mortality, rates, onehot
    )
    summed = month_total(grad_one) + total_two
    return (initial, jnp.stack([sens_one, sens_two], axis=0), summed / cells)


def solution(mesh):
    in_specs = (
        P("ens", "tile", None),
        P("ens", "tile", None),
        P("ens", "tile", None),
        P("ens", None, "tile", None),
        P("ens", None),
        P(),
        P(),
        P("tile", None),
        P("tile", None),
        P("tile", None),
    )
    out_specs = (P("ens", "tile", None), P("ens", None, "tile", None), P("ens", None))
    return jax.shard_map(shards, mesh=mesh, in_specs=in_specs, out_specs=out_specs, check_vma=False)
```

profile of v0, /device:TPU:0, one launch (start us, length us, event | category | flops | bytes accessed | tf_op | source)
XLA Modules:
  0.0 273.3 jit_solution(4688281940485553662)
XLA Ops:
  0.7 0.7 copy-done.40
  1.4 2.4 collective-permute-start.4
  3.8 1.3 collective-permute-start.5
  7.3 0.7 fusion.47
  8.0 0.7 fusion.48
  8.8 2.4 fusion.15
  11.2 2.4 fusion.13
  13.8 0.7 subtract_subtract_fusion
  14.5 94.6 %while.20 = (s32[]{:T(128)}, f32[160,2,1024]{2,1,0:T(2,128)S(1)}, f32[4,1024]{1,0:T(4,128)}, f32[4,1024]{1,0:T(4,128)}, f32[4,1024]{1,0:T(4,128)}, /*index=5*/f32[4,1024]{1,0:T(4,128)}, f32[4,1024]{1,0:T(4,128)}, s32[]{:T(128)}) while((s32[]{:T(128)}, f32[160,2,1024]{2,1,0:T(2,128)S(1)}, f32[4,1024]{1,0:T(4,128)}, f32[4,1024]{1,0:T(4,128)}, ...), condition=%wide.region_1.2_spmd, body=%wide.region_0.1_spmd.sunk | while | flops 4259842 | bytes 22864288 | solution.py:61
  15.0 1.0 fusion.72
  16.1 1.3 collective-permute-start
  17.4 6.6 %collective-permute-start.1 = (f32[160,1,1024]{2,1,0:T(1,128)S(1)}, f32[160,1,1024]{2,1,0:T(1,128)}, u32[]{:S(2)}, u32[]{:S(2)}) collective-permute-start(f32[160,1,1024]{2,1,0:T(1,128)S(1)} %get-tuple-element.228), channel_id=1, source_target_pairs={{0,1},{1,2},{2,3},{3,4},{4,5},{5,6},{6,7},{7,8},{8,9},{9,10},{10,1... | collective-permute-start | bytes 1966088 | tf_op jit(solution)/shard_map/while/body/eval_jaxpr/ppermute | solution.py:18
  26.7 1.8 fusion.74
  28.6 5.9 %fusion.75 = f32[160,2,1024]{2,1,0:T(2,128)S(1)} fusion(f32[160,1,1024]{2,1,0:T(1,128)S(1)} %collective-permute-done, f32[160,2,1024]{2,1,0:T(2,128)S(1)} %copy.37, f32[160,1,1024]{2,1,0:T(1,128)} %collective-permute-done.1, f32[160,2,1]{2,1,0:T(2,128)S(1)} %get-tuple-element.229, f32[160,2,1023]{2,1,0:T(2,128)S(1)} %get-tuple-element.230, ...), kind=kLoop, calls=%fused_computation.4.clone.1 | loop fusion | flops 4259840 | bytes 6594560 | tf_op jit(solution)/shard_map/while/body/eval_jaxpr/add | solution.py:46
  35.0 1.0 fusion.72
  36.1 1.3 collective-permute-start
  37.4 13.3 %collective-permute-start.1 = (f32[160,1,1024]{2,1,0:T(1,128)S(1)}, f32[160,1,1024]{2,1,0:T(1,128)}, u32[]{:S(2)}, u32[]{:S(2)}) collective-permute-start(f32[160,1,1024]{2,1,0:T(1,128)S(1)} %get-tuple-element.228), channel_id=1, source_target_pairs={{0,1},{1,2},{2,3},{3,4},{4,5},{5,6},{6,7},{7,8},{8,9},{9,10},{10,1... | collective-permute-start | bytes 1966088 | tf_op jit(solution)/shard_map/while/body/eval_jaxpr/ppermute | solution.py:18
  53.4 1.8 fusion.74
  55.2 5.9 %fusion.75 = f32[160,2,1024]{2,1,0:T(2,128)S(1)} fusion(f32[160,1,1024]{2,1,0:T(1,128)S(1)} %collective-permute-done, f32[160,2,1024]{2,1,0:T(2,128)S(1)} %copy.37, f32[160,1,1024]{2,1,0:T(1,128)} %collective-permute-done.1, f32[160,2,1]{2,1,0:T(2,128)S(1)} %get-tuple-element.229, f32[160,2,1023]{2,1,0:T(2,128)S(1)} %get-tuple-element.230, ...), kind=kLoop, calls=%fused_computation.4.clone.1 | loop fusion | flops 4259840 | bytes 6594560 | tf_op jit(solution)/shard_map/while/body/eval_jaxpr/add | solution.py:46
  61.7 1.0 fusion.72
  62.7 1.3 collective-permute-start
  64.0 9.1 %collective-permute-start.1 = (f32[160,1,1024]{2,1,0:T(1,128)S(1)}, f32[160,1,1024]{2,1,0:T(1,128)}, u32[]{:S(2)}, u32[]{:S(2)}) collective-permute-start(f32[160,1,1024]{2,1,0:T(1,128)S(1)} %get-tuple-element.228), channel_id=1, source_target_pairs={{0,1},{1,2},{2,3},{3,4},{4,5},{5,6},{6,7},{7,8},{8,9},{9,10},{10,1... | collective-permute-start | bytes 1966088 | tf_op jit(solution)/shard_map/while/body/eval_jaxpr/ppermute | solution.py:18
  75.8 1.8 fusion.74
  77.7 5.9 %fusion.75 = f32[160,2,1024]{2,1,0:T(2,128)S(1)} fusion(f32[160,1,1024]{2,1,0:T(1,128)S(1)} %collective-permute-done, f32[160,2,1024]{2,1,0:T(2,128)S(1)} %copy.37, f32[160,1,1024]{2,1,0:T(1,128)} %collective-permute-done.1, f32[160,2,1]{2,1,0:T(2,128)S(1)} %get-tuple-element.229, f32[160,2,1023]{2,1,0:T(2,128)S(1)} %get-tuple-element.230, ...), kind=kLoop, calls=%fused_computation.4.clone.1 | loop fusion | flops 4259840 | bytes 6594560 | tf_op jit(solution)/shard_map/while/body/eval_jaxpr/add | solution.py:46
  84.2 1.0 fusion.72
  85.2 1.3 collective-permute-start
  86.5 12.1 %collective-permute-start.1 = (f32[160,1,1024]{2,1,0:T(1,128)S(1)}, f32[160,1,1024]{2,1,0:T(1,128)}, u32[]{:S(2)}, u32[]{:S(2)}) collective-permute-start(f32[160,1,1024]{2,1,0:T(1,128)S(1)} %get-tuple-element.228), channel_id=1, source_target_pairs={{0,1},{1,2},{2,3},{3,4},{4,5},{5,6},{6,7},{7,8},{8,9},{9,10},{10,1... | collective-permute-start | bytes 1966088 | tf_op jit(solution)/shard_map/while/body/eval_jaxpr/ppermute | solution.py:18
  101.4 1.8 fusion.74
  103.2 5.9 %fusion.75 = f32[160,2,1024]{2,1,0:T(2,128)S(1)} fusion(f32[160,1,1024]{2,1,0:T(1,128)S(1)} %collective-permute-done, f32[160,2,1024]{2,1,0:T(2,128)S(1)} %copy.37, f32[160,1,1024]{2,1,0:T(1,128)} %collective-permute-done.1, f32[160,2,1]{2,1,0:T(2,128)S(1)} %get-tuple-element.229, f32[160,2,1023]{2,1,0:T(2,128)S(1)} %get-tuple-element.230, ...), kind=kLoop, calls=%fused_computation.4.clone.1 | loop fusion | flops 4259840 | bytes 6594560 | tf_op jit(solution)/shard_map/while/body/eval_jaxpr/add | solution.py:46
  110.7 0.8 copy-done.5
  111.9 1.8 fusion.31
  113.7 1.5 multiply_divide_fusion
  115.9 1.4 convolution_add_fusion.2
  117.2 1.1 reshape.61
  118.4 96.1 %while.21 = (s32[]{:T(128)}, f32[160,2,1024]{2,1,0:T(2,128)S(1)}, f32[4,1024]{1,0:T(4,128)}, f32[4,1024]{1,0:T(4,128)}, f32[4,1024]{1,0:T(4,128)}, /*index=5*/f32[4,1024]{1,0:T(4,128)}, f32[4,1024]{1,0:T(4,128)}, s32[]{:T(128)}) while((s32[]{:T(128)}, f32[160,2,1024]{2,1,0:T(2,128)S(1)}, f32[4,1024]{1,0:T(4,128)}, f32[4,1024]{1,0:T(4,128)}, ...), condition=%wide.region_3.4_spmd, body=%wide.region_2.3_spmd.sunk | while | flops 4259842 | bytes 22864288 | solution.py:61
  119.1 1.0 fusion.76
  120.1 1.3 collective-permute-start.2
  121.4 9.1 %collective-permute-start.3 = (f32[160,1,1024]{2,1,0:T(1,128)S(1)}, f32[160,1,1024]{2,1,0:T(1,128)}, u32[]{:S(2)}, u32[]{:S(2)}) collective-permute-start(f32[160,1,1024]{2,1,0:T(1,128)S(1)} %get-tuple-element.241), channel_id=1, source_target_pairs={{0,1},{1,2},{2,3},{3,4},{4,5},{5,6},{6,7},{7,8},{8,9},{9,10},{10,1... | collective-permute-start | bytes 1966088 | tf_op jit(solution)/shard_map/while/body/eval_jaxpr/ppermute | solution.py:18
  133.2 1.8 fusion.78
  135.1 5.9 %fusion.79 = f32[160,2,1024]{2,1,0:T(2,128)S(1)} fusion(f32[160,1,1024]{2,1,0:T(1,128)S(1)} %collective-permute-done.2, f32[160,2,1024]{2,1,0:T(2,128)S(1)} %copy.38, f32[160,1,1024]{2,1,0:T(1,128)} %collective-permute-done.3, f32[160,2,1]{2,1,0:T(2,128)S(1)} %get-tuple-element.242, f32[160,2,1023]{2,1,0:T(2,128)S(1)} %get-tuple-element.243, ...), kind=kLoop, calls=%fused_computation.14.clone.1 | loop fusion | flops 4259840 | bytes 6594560 | tf_op jit(solution)/shard_map/while/body/eval_jaxpr/add | solution.py:46
  141.5 1.0 fusion.76
  142.6 1.3 collective-permute-start.2
  143.9 12.2 %collective-permute-start.3 = (f32[160,1,1024]{2,1,0:T(1,128)S(1)}, f32[160,1,1024]{2,1,0:T(1,128)}, u32[]{:S(2)}, u32[]{:S(2)}) collective-permute-start(f32[160,1,1024]{2,1,0:T(1,128)S(1)} %get-tuple-element.241), channel_id=1, source_target_pairs={{0,1},{1,2},{2,3},{3,4},{4,5},{5,6},{6,7},{7,8},{8,9},{9,10},{10,1... | collective-permute-start | bytes 1966088 | tf_op jit(solution)/shard_map/while/body/eval_jaxpr/ppermute | solution.py:18
  158.7 1.8 fusion.78
  160.6 5.9 %fusion.79 = f32[160,2,1024]{2,1,0:T(2,128)S(1)} fusion(f32[160,1,1024]{2,1,0:T(1,128)S(1)} %collective-permute-done.2, f32[160,2,1024]{2,1,0:T(2,128)S(1)} %copy.38, f32[160,1,1024]{2,1,0:T(1,128)} %collective-permute-done.3, f32[160,2,1]{2,1,0:T(2,128)S(1)} %get-tuple-element.242, f32[160,2,1023]{2,1,0:T(2,128)S(1)} %get-tuple-element.243, ...), kind=kLoop, calls=%fused_computation.14.clone.1 | loop fusion | flops 4259840 | bytes 6594560 | tf_op jit(solution)/shard_map/while/body/eval_jaxpr/add | solution.py:46
  167.1 1.0 fusion.76
  168.1 1.3 collective-permute-start.2
  169.4 9.2 %collective-permute-start.3 = (f32[160,1,1024]{2,1,0:T(1,128)S(1)}, f32[160,1,1024]{2,1,0:T(1,128)}, u32[]{:S(2)}, u32[]{:S(2)}) collective-permute-start(f32[160,1,1024]{2,1,0:T(1,128)S(1)} %get-tuple-element.241), channel_id=1, source_target_pairs={{0,1},{1,2},{2,3},{3,4},{4,5},{5,6},{6,7},{7,8},{8,9},{9,10},{10,1... | collective-permute-start | bytes 1966088 | tf_op jit(solution)/shard_map/while/body/eval_jaxpr/ppermute | solution.py:18
  181.3 1.8 fusion.78
  183.1 5.9 %fusion.79 = f32[160,2,1024]{2,1,0:T(2,128)S(1)} fusion(f32[160,1,1024]{2,1,0:T(1,128)S(1)} %collective-permute-done.2, f32[160,2,1024]{2,1,0:T(2,128)S(1)} %copy.38, f32[160,1,1024]{2,1,0:T(1,128)} %collective-permute-done.3, f32[160,2,1]{2,1,0:T(2,128)S(1)} %get-tuple-element.242, f32[160,2,1023]{2,1,0:T(2,128)S(1)} %get-tuple-element.243, ...), kind=kLoop, calls=%fused_computation.14.clone.1 | loop fusion | flops 4259840 | bytes 6594560 | tf_op jit(solution)/shard_map/while/body/eval_jaxpr/add | solution.py:46
  189.6 1.0 fusion.76
  190.6 1.3 collective-permute-start.2
  191.9 12.1 %collective-permute-start.3 = (f32[160,1,1024]{2,1,0:T(1,128)S(1)}, f32[160,1,1024]{2,1,0:T(1,128)}, u32[]{:S(2)}, u32[]{:S(2)}) collective-permute-start(f32[160,1,1024]{2,1,0:T(1,128)S(1)} %get-tuple-element.241), channel_id=1, source_target_pairs={{0,1},{1,2},{2,3},{3,4},{4,5},{5,6},{6,7},{7,8},{8,9},{9,10},{10,1... | collective-permute-start | bytes 1966088 | tf_op jit(solution)/shard_map/while/body/eval_jaxpr/ppermute | solution.py:18
  206.7 1.8 fusion.78
  208.5 5.9 %fusion.79 = f32[160,2,1024]{2,1,0:T(2,128)S(1)} fusion(f32[160,1,1024]{2,1,0:T(1,128)S(1)} %collective-permute-done.2, f32[160,2,1024]{2,1,0:T(2,128)S(1)} %copy.38, f32[160,1,1024]{2,1,0:T(1,128)} %collective-permute-done.3, f32[160,2,1]{2,1,0:T(2,128)S(1)} %get-tuple-element.242, f32[160,2,1023]{2,1,0:T(2,128)S(1)} %get-tuple-element.243, ...), kind=kLoop, calls=%fused_computation.14.clone.1 | loop fusion | flops 4259840 | bytes 6594560 | tf_op jit(solution)/shard_map/while/body/eval_jaxpr/add | solution.py:46
  216.0 0.8 copy-done.3
  217.3 1.2 fusion.32
  218.5 0.8 multiply_divide_fusion.1
  219.8 1.2 fusion.16
  221.0 1.4 convolution_add_fusion
  222.3 1.2 fusion.17
  224.0 45.8 %psum.16 = f32[16,6]{0,1:T(8,128)S(1)} all-reduce(f32[16,6]{0,1:T(8,128)S(1)} %convolution_add_fusion.4), channel_id=1, replica_groups=mesh['ens'=2,'tile'=16] {'tile'}, use_global_device_ids=true, to_apply=%region_4.5 | all-reduce | flops 96 | bytes 768 | tf_op jit(solution)/shard_map/psum | solution.py:115
  270.4 2.2 reshape.64
  272.6 0.7 pad_maximum_fusion.6
  (287 shorter events, 33.5 us)
Async XLA Ops:
  0.6 6.3 %copy-start = (f32[16,6]{0,1:T(8,128)S(1)}, f32[16,6]{0,1:T(8,128)}, u32[]{:S(2)}) copy-start(f32[16,6]{0,1:T(8,128)} %param.18) | copy-start | bytes 1156
  0.7 4.4 %copy-start.9 = (f32[160,2,1024]{2,1,0:T(2,128)S(1)}, f32[160,2,1024]{2,1,0:T(2,128)}, u32[]{:S(2)}) copy-start(f32[160,2,1024]{2,1,0:T(2,128)} %param.16) | copy-start | bytes 3932164
  1.4 12.2 %collective-permute-start.4 = (f32[3,2,1024]{2,1,0:T(2,128)S(1)}, f32[3,2,1024]{2,1,0:T(2,128)S(1)}, u32[]{:S(2)}, u32[]{:S(2)}) collective-permute-start(f32[3,2,1024]{2,1,0:T(2,128)S(1)} %pad_maximum_fusion.7), channel_id=1, source_target_pairs={{0,1},{1,2},{2,3},{3,4},{4,5},{5,6},{6,7},{7,8},{8,9},{9,10},{10,1... | collective-permute-start | bytes 73736 | tf_op jit(solution)/shard_map/ppermute | solution.py:18
  3.8 9.8 %collective-permute-start.5 = (f32[3,2,1024]{2,1,0:T(2,128)S(1)}, f32[3,2,1024]{2,1,0:T(2,128)S(1)}, u32[]{:S(2)}, u32[]{:S(2)}) collective-permute-start(f32[3,2,1024]{2,1,0:T(2,128)S(1)} %pad_maximum_fusion.7), channel_id=1, source_target_pairs={{1,0},{2,1},{3,2},{4,3},{5,4},{6,5},{7,6},{8,7},{9,8},{10,9},{11,1... | collective-permute-start | bytes 73736 | tf_op jit(solution)/shard_map/ppermute | solution.py:20
  7.3 3.9 %copy-start.19 = (f32[160,6]{0,1:T(8,128)}, f32[160,6]{0,1:T(8,128)S(1)}, u32[]{:S(2)}) copy-start(f32[160,6]{0,1:T(8,128)S(1)} %fusion.27) | copy-start | bytes 11524
  8.8 5.7 %copy-start.1 = (f32[160,2,1024]{2,1,0:T(2,128)S(1)}, f32[160,2,1024]{2,1,0:T(2,128)}, u32[]{:S(2)}) copy-start(f32[160,2,1024]{2,1,0:T(2,128)} %param.14) | copy-start | bytes 3932164
  15.0 9.0 %copy-start.32 = (f32[4,1024]{1,0:T(4,128)S(1)}, f32[4,1024]{1,0:T(4,128)}, u32[]{:S(2)}) copy-start(f32[4,1024]{1,0:T(4,128)} %get-tuple-element.268) | copy-start | bytes 49156 | tf_op jit(solution)/shard_map/while
  15.0 9.0 %copy-start.30 = (f32[4,1024]{1,0:T(4,128)S(1)}, f32[4,1024]{1,0:T(4,128)}, u32[]{:S(2)}) copy-start(f32[4,1024]{1,0:T(4,128)} %get-tuple-element.267) | copy-start | bytes 49156 | tf_op jit(solution)/shard_map/while
  15.0 9.6 %copy-start.28 = (f32[4,1024]{1,0:T(4,128)S(1)}, f32[4,1024]{1,0:T(4,128)}, u32[]{:S(2)}) copy-start(f32[4,1024]{1,0:T(4,128)} %get-tuple-element.266) | copy-start | bytes 49156 | tf_op jit(solution)/shard_map/while
  15.0 10.2 %copy-start.26 = (f32[4,1024]{1,0:T(4,128)S(1)}, f32[4,1024]{1,0:T(4,128)}, u32[]{:S(2)}) copy-start(f32[4,1024]{1,0:T(4,128)} %get-tuple-element.265) | copy-start | bytes 49156 | tf_op jit(solution)/shard_map/while
  15.0 10.8 %copy-start.24 = (f32[4,1024]{1,0:T(4,128)S(1)}, f32[4,1024]{1,0:T(4,128)}, u32[]{:S(2)}) copy-start(f32[4,1024]{1,0:T(4,128)} %get-tuple-element.264) | copy-start | bytes 49156 | tf_op jit(solution)/shard_map/while
  16.1 12.4 %collective-permute-start = (f32[160,1,1024]{2,1,0:T(1,128)S(1)}, f32[160,1,1024]{2,1,0:T(1,128)S(1)}, u32[]{:S(2)}, u32[]{:S(2)}) collective-permute-start(f32[160,1,1024]{2,1,0:T(1,128)S(1)} %get-tuple-element.227), channel_id=1, source_target_pairs={{1,0},{2,1},{3,2},{4,3},{5,4},{6,5},{7,6},{8,7},{9,8},{10,9},{11,1... | collective-permute-start | bytes 1966088 | tf_op jit(solution)/shard_map/while/body/eval_jaxpr/ppermute | solution.py:20
  17.4 11.2 %collective-permute-start.1 = (f32[160,1,1024]{2,1,0:T(1,128)S(1)}, f32[160,1,1024]{2,1,0:T(1,128)}, u32[]{:S(2)}, u32[]{:S(2)}) collective-permute-start(f32[160,1,1024]{2,1,0:T(1,128)S(1)} %get-tuple-element.228), channel_id=1, source_target_pairs={{0,1},{1,2},{2,3},{3,4},{4,5},{5,6},{6,7},{7,8},{8,9},{9,10},{10,1... | collective-permute-start | bytes 1966088 | tf_op jit(solution)/shard_map/while/body/eval_jaxpr/ppermute | solution.py:18
  35.0 15.7 %copy-start.32 = (f32[4,1024]{1,0:T(4,128)S(1)}, f32[4,1024]{1,0:T(4,128)}, u32[]{:S(2)}) copy-start(f32[4,1024]{1,0:T(4,128)} %get-tuple-element.268) | copy-start | bytes 49156 | tf_op jit(solution)/shard_map/while
  35.0 15.7 %copy-start.30 = (f32[4,1024]{1,0:T(4,128)S(1)}, f32[4,1024]{1,0:T(4,128)}, u32[]{:S(2)}) copy-start(f32[4,1024]{1,0:T(4,128)} %get-tuple-element.267) | copy-start | bytes 49156 | tf_op jit(solution)/shard_map/while
  35.0 16.3 %copy-start.28 = (f32[4,1024]{1,0:T(4,128)S(1)}, f32[4,1024]{1,0:T(4,128)}, u32[]{:S(2)}) copy-start(f32[4,1024]{1,0:T(4,128)} %get-tuple-element.266) | copy-start | bytes 49156 | tf_op jit(solution)/shard_map/while
  35.0 16.9 %copy-start.26 = (f32[4,1024]{1,0:T(4,128)S(1)}, f32[4,1024]{1,0:T(4,128)}, u32[]{:S(2)}) copy-start(f32[4,1024]{1,0:T(4,128)} %get-tuple-element.265) | copy-start | bytes 49156 | tf_op jit(solution)/shard_map/while
  35.0 17.5 %copy-start.24 = (f32[4,1024]{1,0:T(4,128)S(1)}, f32[4,1024]{1,0:T(4,128)}, u32[]{:S(2)}) copy-start(f32[4,1024]{1,0:T(4,128)} %get-tuple-element.264) | copy-start | bytes 49156 | tf_op jit(solution)/shard_map/while
  36.1 19.1 %collective-permute-start = (f32[160,1,1024]{2,1,0:T(1,128)S(1)}, f32[160,1,1024]{2,1,0:T(1,128)S(1)}, u32[]{:S(2)}, u32[]{:S(2)}) collective-permute-start(f32[160,1,1024]{2,1,0:T(1,128)S(1)} %get-tuple-element.227), channel_id=1, source_target_pairs={{1,0},{2,1},{3,2},{4,3},{5,4},{6,5},{7,6},{8,7},{9,8},{10,9},{11,1... | collective-permute-start | bytes 1966088 | tf_op jit(solution)/shard_map/while/body/eval_jaxpr/ppermute | solution.py:20
  37.4 17.8 %collective-permute-start.1 = (f32[160,1,1024]{2,1,0:T(1,128)S(1)}, f32[160,1,1024]{2,1,0:T(1,128)}, u32[]{:S(2)}, u32[]{:S(2)}) collective-permute-start(f32[160,1,1024]{2,1,0:T(1,128)S(1)} %get-tuple-element.228), channel_id=1, source_target_pairs={{0,1},{1,2},{2,3},{3,4},{4,5},{5,6},{6,7},{7,8},{8,9},{9,10},{10,1... | collective-permute-start | bytes 1966088 | tf_op jit(solution)/shard_map/while/body/eval_jaxpr/ppermute | solution.py:18
  53.4 1.9 copy-start.11
  61.7 11.5 %copy-start.32 = (f32[4,1024]{1,0:T(4,128)S(1)}, f32[4,1024]{1,0:T(4,128)}, u32[]{:S(2)}) copy-start(f32[4,1024]{1,0:T(4,128)} %get-tuple-element.268) | copy-start | bytes 49156 | tf_op jit(solution)/shard_map/while
  61.7 11.5 %copy-start.30 = (f32[4,1024]{1,0:T(4,128)S(1)}, f32[4,1024]{1,0:T(4,128)}, u32[]{:S(2)}) copy-start(f32[4,1024]{1,0:T(4,128)} %get-tuple-element.267) | copy-start | bytes 49156 | tf_op jit(solution)/shard_map/while
  61.7 12.1 %copy-start.28 = (f32[4,1024]{1,0:T(4,128)S(1)}, f32[4,1024]{1,0:T(4,128)}, u32[]{:S(2)}) copy-start(f32[4,1024]{1,0:T(4,128)} %get-tuple-element.266) | copy-start | bytes 49156 | tf_op jit(solution)/shard_map/while
  61.7 12.7 %copy-start.26 = (f32[4,1024]{1,0:T(4,128)S(1)}, f32[4,1024]{1,0:T(4,128)}, u32[]{:S(2)}) copy-start(f32[4,1024]{1,0:T(4,128)} %get-tuple-element.265) | copy-start | bytes 49156 | tf_op jit(solution)/shard_map/while
  61.7 13.3 %copy-start.24 = (f32[4,1024]{1,0:T(4,128)S(1)}, f32[4,1024]{1,0:T(4,128)}, u32[]{:S(2)}) copy-start(f32[4,1024]{1,0:T(4,128)} %get-tuple-element.264) | copy-start | bytes 49156 | tf_op jit(solution)/shard_map/while
  62.7 14.9 %collective-permute-start = (f32[160,1,1024]{2,1,0:T(1,128)S(1)}, f32[160,1,1024]{2,1,0:T(1,128)S(1)}, u32[]{:S(2)}, u32[]{:S(2)}) collective-permute-start(f32[160,1,1024]{2,1,0:T(1,128)S(1)} %get-tuple-element.227), channel_id=1, source_target_pairs={{1,0},{2,1},{3,2},{4,3},{5,4},{6,5},{7,6},{8,7},{9,8},{10,9},{11,1... | collective-permute-start | bytes 1966088 | tf_op jit(solution)/shard_map/while/body/eval_jaxpr/ppermute | solution.py:20
  64.0 13.6 %collective-permute-start.1 = (f32[160,1,1024]{2,1,0:T(1,128)S(1)}, f32[160,1,1024]{2,1,0:T(1,128)}, u32[]{:S(2)}, u32[]{:S(2)}) collective-permute-start(f32[160,1,1024]{2,1,0:T(1,128)S(1)} %get-tuple-element.228), channel_id=1, source_target_pairs={{0,1},{1,2},{2,3},{3,4},{4,5},{5,6},{6,7},{7,8},{8,9},{9,10},{10,1... | collective-permute-start | bytes 1966088 | tf_op jit(solution)/shard_map/while/body/eval_jaxpr/ppermute | solution.py:18
  84.1 14.5 %copy-start.32 = (f32[4,1024]{1,0:T(4,128)S(1)}, f32[4,1024]{1,0:T(4,128)}, u32[]{:S(2)}) copy-start(f32[4,1024]{1,0:T(4,128)} %get-tuple-element.268) | copy-start | bytes 49156 | tf_op jit(solution)/shard_map/while
  84.1 14.5 %copy-start.30 = (f32[4,1024]{1,0:T(4,128)S(1)}, f32[4,1024]{1,0:T(4,128)}, u32[]{:S(2)}) copy-start(f32[4,1024]{1,0:T(4,128)} %get-tuple-element.267) | copy-start | bytes 49156 | tf_op jit(solution)/shard_map/while
  84.2 15.1 %copy-start.28 = (f32[4,1024]{1,0:T(4,128)S(1)}, f32[4,1024]{1,0:T(4,128)}, u32[]{:S(2)}) copy-start(f32[4,1024]{1,0:T(4,128)} %get-tuple-element.266) | copy-start | bytes 49156 | tf_op jit(solution)/shard_map/while
  84.2 15.7 %copy-start.26 = (f32[4,1024]{1,0:T(4,128)S(1)}, f32[4,1024]{1,0:T(4,128)}, u32[]{:S(2)}) copy-start(f32[4,1024]{1,0:T(4,128)} %get-tuple-element.265) | copy-start | bytes 49156 | tf_op jit(solution)/shard_map/while
  84.2 16.3 %copy-start.24 = (f32[4,1024]{1,0:T(4,128)S(1)}, f32[4,1024]{1,0:T(4,128)}, u32[]{:S(2)}) copy-start(f32[4,1024]{1,0:T(4,128)} %get-tuple-element.264) | copy-start | bytes 49156 | tf_op jit(solution)/shard_map/while
  85.2 17.9 %collective-permute-start = (f32[160,1,1024]{2,1,0:T(1,128)S(1)}, f32[160,1,1024]{2,1,0:T(1,128)S(1)}, u32[]{:S(2)}, u32[]{:S(2)}) collective-permute-start(f32[160,1,1024]{2,1,0:T(1,128)S(1)} %get-tuple-element.227), channel_id=1, source_target_pairs={{1,0},{2,1},{3,2},{4,3},{5,4},{6,5},{7,6},{8,7},{9,8},{10,9},{11,1... | collective-permute-start | bytes 1966088 | tf_op jit(solution)/shard_map/while/body/eval_jaxpr/ppermute | solution.py:20
  86.5 16.7 %collective-permute-start.1 = (f32[160,1,1024]{2,1,0:T(1,128)S(1)}, f32[160,1,1024]{2,1,0:T(1,128)}, u32[]{:S(2)}, u32[]{:S(2)}) collective-permute-start(f32[160,1,1024]{2,1,0:T(1,128)S(1)} %get-tuple-element.228), channel_id=1, source_target_pairs={{0,1},{1,2},{2,3},{3,4},{4,5},{5,6},{6,7},{7,8},{8,9},{9,10},{10,1... | collective-permute-start | bytes 1966088 | tf_op jit(solution)/shard_map/while/body/eval_jaxpr/ppermute | solution.py:18
  119.0 11.5 %copy-start.33 = (f32[4,1024]{1,0:T(4,128)S(1)}, f32[4,1024]{1,0:T(4,128)}, u32[]{:S(2)}) copy-start(f32[4,1024]{1,0:T(4,128)} %get-tuple-element.292) | copy-start | bytes 49156 | tf_op jit(solution)/shard_map/while
  119.1 11.5 %copy-start.31 = (f32[4,1024]{1,0:T(4,128)S(1)}, f32[4,1024]{1,0:T(4,128)}, u32[]{:S(2)}) copy-start(f32[4,1024]{1,0:T(4,128)} %get-tuple-element.291) | copy-start | bytes 49156 | tf_op jit(solution)/shard_map/while
  119.1 12.1 %copy-start.29 = (f32[4,1024]{1,0:T(4,128)S(1)}, f32[4,1024]{1,0:T(4,128)}, u32[]{:S(2)}) copy-start(f32[4,1024]{1,0:T(4,128)} %get-tuple-element.290) | copy-start | bytes 49156 | tf_op jit(solution)/shard_map/while
  119.1 12.7 %copy-start.27 = (f32[4,1024]{1,0:T(4,128)S(1)}, f32[4,1024]{1,0:T(4,128)}, u32[]{:S(2)}) copy-start(f32[4,1024]{1,0:T(4,128)} %get-tuple-element.289) | copy-start | bytes 49156 | tf_op jit(solution)/shard_map/while
  119.1 13.3 %copy-start.25 = (f32[4,1024]{1,0:T(4,128)S(1)}, f32[4,1024]{1,0:T(4,128)}, u32[]{:S(2)}) copy-start(f32[4,1024]{1,0:T(4,128)} %get-tuple-element.288) | copy-start | bytes 49156 | tf_op jit(solution)/shard_map/while
  120.1 14.9 %collective-permute-start.2 = (f32[160,1,1024]{2,1,0:T(1,128)S(1)}, f32[160,1,1024]{2,1,0:T(1,128)S(1)}, u32[]{:S(2)}, u32[]{:S(2)}) collective-permute-start(f32[160,1,1024]{2,1,0:T(1,128)S(1)} %get-tuple-element.240), channel_id=1, source_target_pairs={{1,0},{2,1},{3,2},{4,3},{5,4},{6,5},{7,6},{8,7},{9,8},{10,9},{11,1... | collective-permute-start | bytes 1966088 | tf_op jit(solution)/shard_map/while/body/eval_jaxpr/ppermute | solution.py:20
  121.4 13.6 %collective-permute-start.3 = (f32[160,1,1024]{2,1,0:T(1,128)S(1)}, f32[160,1,1024]{2,1,0:T(1,128)}, u32[]{:S(2)}, u32[]{:S(2)}) collective-permute-start(f32[160,1,1024]{2,1,0:T(1,128)S(1)} %get-tuple-element.241), channel_id=1, source_target_pairs={{0,1},{1,2},{2,3},{3,4},{4,5},{5,6},{6,7},{7,8},{8,9},{9,10},{10,1... | collective-permute-start | bytes 1966088 | tf_op jit(solution)/shard_map/while/body/eval_jaxpr/ppermute | solution.py:18
  141.5 14.5 %copy-start.33 = (f32[4,1024]{1,0:T(4,128)S(1)}, f32[4,1024]{1,0:T(4,128)}, u32[]{:S(2)}) copy-start(f32[4,1024]{1,0:T(4,128)} %get-tuple-element.292) | copy-start | bytes 49156 | tf_op jit(solution)/shard_map/while
  141.5 14.5 %copy-start.31 = (f32[4,1024]{1,0:T(4,128)S(1)}, f32[4,1024]{1,0:T(4,128)}, u32[]{:S(2)}) copy-start(f32[4,1024]{1,0:T(4,128)} %get-tuple-element.291) | copy-start | bytes 49156 | tf_op jit(solution)/shard_map/while
  141.5 15.1 %copy-start.29 = (f32[4,1024]{1,0:T(4,128)S(1)}, f32[4,1024]{1,0:T(4,128)}, u32[]{:S(2)}) copy-start(f32[4,1024]{1,0:T(4,128)} %get-tuple-element.290) | copy-start | bytes 49156 | tf_op jit(solution)/shard_map/while
  141.5 15.7 %copy-start.27 = (f32[4,1024]{1,0:T(4,128)S(1)}, f32[4,1024]{1,0:T(4,128)}, u32[]{:S(2)}) copy-start(f32[4,1024]{1,0:T(4,128)} %get-tuple-element.289) | copy-start | bytes 49156 | tf_op jit(solution)/shard_map/while
  141.5 16.3 %copy-start.25 = (f32[4,1024]{1,0:T(4,128)S(1)}, f32[4,1024]{1,0:T(4,128)}, u32[]{:S(2)}) copy-start(f32[4,1024]{1,0:T(4,128)} %get-tuple-element.288) | copy-start | bytes 49156 | tf_op jit(solution)/shard_map/while
  142.6 17.9 %collective-permute-start.2 = (f32[160,1,1024]{2,1,0:T(1,128)S(1)}, f32[160,1,1024]{2,1,0:T(1,128)S(1)}, u32[]{:S(2)}, u32[]{:S(2)}) collective-permute-start(f32[160,1,1024]{2,1,0:T(1,128)S(1)} %get-tuple-element.240), channel_id=1, source_target_pairs={{1,0},{2,1},{3,2},{4,3},{5,4},{6,5},{7,6},{8,7},{9,8},{10,9},{11,1... | collective-permute-start | bytes 1966088 | tf_op jit(solution)/shard_map/while/body/eval_jaxpr/ppermute | solution.py:20
  143.9 16.7 %collective-permute-start.3 = (f32[160,1,1024]{2,1,0:T(1,128)S(1)}, f32[160,1,1024]{2,1,0:T(1,128)}, u32[]{:S(2)}, u32[]{:S(2)}) collective-permute-start(f32[160,1,1024]{2,1,0:T(1,128)S(1)} %get-tuple-element.241), channel_id=1, source_target_pairs={{0,1},{1,2},{2,3},{3,4},{4,5},{5,6},{6,7},{7,8},{8,9},{9,10},{10,1... | collective-permute-start | bytes 1966088 | tf_op jit(solution)/shard_map/while/body/eval_jaxpr/ppermute | solution.py:18
  167.0 11.6 %copy-start.33 = (f32[4,1024]{1,0:T(4,128)S(1)}, f32[4,1024]{1,0:T(4,128)}, u32[]{:S(2)}) copy-start(f32[4,1024]{1,0:T(4,128)} %get-tuple-element.292) | copy-start | bytes 49156 | tf_op jit(solution)/shard_map/while
  167.0 11.6 %copy-start.31 = (f32[4,1024]{1,0:T(4,128)S(1)}, f32[4,1024]{1,0:T(4,128)}, u32[]{:S(2)}) copy-start(f32[4,1024]{1,0:T(4,128)} %get-tuple-element.291) | copy-start | bytes 49156 | tf_op jit(solution)/shard_map/while
  167.0 12.2 %copy-start.29 = (f32[4,1024]{1,0:T(4,128)S(1)}, f32[4,1024]{1,0:T(4,128)}, u32[]{:S(2)}) copy-start(f32[4,1024]{1,0:T(4,128)} %get-tuple-element.290) | copy-start | bytes 49156 | tf_op jit(solution)/shard_map/while
  167.0 12.8 %copy-start.27 = (f32[4,1024]{1,0:T(4,128)S(1)}, f32[4,1024]{1,0:T(4,128)}, u32[]{:S(2)}) copy-start(f32[4,1024]{1,0:T(4,128)} %get-tuple-element.289) | copy-start | bytes 49156 | tf_op jit(solution)/shard_map/while
  167.0 13.4 %copy-start.25 = (f32[4,1024]{1,0:T(4,128)S(1)}, f32[4,1024]{1,0:T(4,128)}, u32[]{:S(2)}) copy-start(f32[4,1024]{1,0:T(4,128)} %get-tuple-element.288) | copy-start | bytes 49156 | tf_op jit(solution)/shard_map/while
  168.1 15.0 %collective-permute-start.2 = (f32[160,1,1024]{2,1,0:T(1,128)S(1)}, f32[160,1,1024]{2,1,0:T(1,128)S(1)}, u32[]{:S(2)}, u32[]{:S(2)}) collective-permute-start(f32[160,1,1024]{2,1,0:T(1,128)S(1)} %get-tuple-element.240), channel_id=1, source_target_pairs={{1,0},{2,1},{3,2},{4,3},{5,4},{6,5},{7,6},{8,7},{9,8},{10,9},{11,1... | collective-permute-start | bytes 1966088 | tf_op jit(solution)/shard_map/while/body/eval_jaxpr/ppermute | solution.py:20
  169.4 13.7 %collective-permute-start.3 = (f32[160,1,1024]{2,1,0:T(1,128)S(1)}, f32[160,1,1024]{2,1,0:T(1,128)}, u32[]{:S(2)}, u32[]{:S(2)}) collective-permute-start(f32[160,1,1024]{2,1,0:T(1,128)S(1)} %get-tuple-element.241), channel_id=1, source_target_pairs={{0,1},{1,2},{2,3},{3,4},{4,5},{5,6},{6,7},{7,8},{8,9},{9,10},{10,1... | collective-permute-start | bytes 1966088 | tf_op jit(solution)/shard_map/while/body/eval_jaxpr/ppermute | solution.py:18
  189.6 14.4 %copy-start.33 = (f32[4,1024]{1,0:T(4,128)S(1)}, f32[4,1024]{1,0:T(4,128)}, u32[]{:S(2)}) copy-start(f32[4,1024]{1,0:T(4,128)} %get-tuple-element.292) | copy-start | bytes 49156 | tf_op jit(solution)/shard_map/while
  189.6 14.4 %copy-start.31 = (f32[4,1024]{1,0:T(4,128)S(1)}, f32[4,1024]{1,0:T(4,128)}, u32[]{:S(2)}) copy-start(f32[4,1024]{1,0:T(4,128)} %get-tuple-element.291) | copy-start | bytes 49156 | tf_op jit(solution)/shard_map/while
  189.6 15.0 %copy-start.29 = (f32[4,1024]{1,0:T(4,128)S(1)}, f32[4,1024]{1,0:T(4,128)}, u32[]{:S(2)}) copy-start(f32[4,1024]{1,0:T(4,128)} %get-tuple-element.290) | copy-start | bytes 49156 | tf_op jit(solution)/shard_map/while
  189.6 15.6 %copy-start.27 = (f32[4,1024]{1,0:T(4,128)S(1)}, f32[4,1024]{1,0:T(4,128)}, u32[]{:S(2)}) copy-start(f32[4,1024]{1,0:T(4,128)} %get-tuple-element.289) | copy-start | bytes 49156 | tf_op jit(solution)/shard_map/while
  189.6 16.2 %copy-start.25 = (f32[4,1024]{1,0:T(4,128)S(1)}, f32[4,1024]{1,0:T(4,128)}, u32[]{:S(2)}) copy-start(f32[4,1024]{1,0:T(4,128)} %get-tuple-element.288) | copy-start | bytes 49156 | tf_op jit(solution)/shard_map/while
  190.6 17.8 %collective-permute-start.2 = (f32[160,1,1024]{2,1,0:T(1,128)S(1)}, f32[160,1,1024]{2,1,0:T(1,128)S(1)}, u32[]{:S(2)}, u32[]{:S(2)}) collective-permute-start(f32[160,1,1024]{2,1,0:T(1,128)S(1)} %get-tuple-element.240), channel_id=1, source_target_pairs={{1,0},{2,1},{3,2},{4,3},{5,4},{6,5},{7,6},{8,7},{9,8},{10,9},{11,1... | collective-permute-start | bytes 1966088 | tf_op jit(solution)/shard_map/while/body/eval_jaxpr/ppermute | solution.py:20
  191.9 16.6 %collective-permute-start.3 = (f32[160,1,1024]{2,1,0:T(1,128)S(1)}, f32[160,1,1024]{2,1,0:T(1,128)}, u32[]{:S(2)}, u32[]{:S(2)}) collective-permute-start(f32[160,1,1024]{2,1,0:T(1,128)S(1)} %get-tuple-element.241), channel_id=1, source_target_pairs={{0,1},{1,2},{2,3},{3,4},{4,5},{5,6},{6,7},{7,8},{8,9},{9,10},{10,1... | collective-permute-start | bytes 1966088 | tf_op jit(solution)/shard_map/while/body/eval_jaxpr/ppermute | solution.py:18
  222.3 48.1 %copy-start.35 = (f32[6,2048]{1,0:T(8,128)S(1)}, f32[6,2048]{1,0:T(8,128)}, u32[]{:S(2)}) copy-start(f32[6,2048]{1,0:T(8,128)} %get-tuple-element.132) | copy-start | bytes 147460
  (50 other events, 80.6 us)
where the time goes:
time: 274 us; the launch traced here: 273 us
  starting transfers between devices  97.7 us (36%)
  local copies, waits for them, and re-layouts  59.1 us (22%)
  other arithmetic  50.8 us (19%)
  blocking collectives  45.8 us (17%)
  matrix products  17.2 us (6%)
    ppermute x9, starting transfers between devices, with_halo(): lax.ppermute(tail, axis, [(i, (i + 1) % count) for i in range(ends)])  86.1 us
    add x8, other arithmetic, transpose_step(): keep * centre + rate_n * padded[:, :-2] + rate_s * padded[:, 2:]  47.6 us
    psum x1, blocking collectives, month_total(): return lax.psum(local_grad, 'tile')  45.8 us
    slice x40, local copies, waits for them, and re-layouts, transpose_step(): r[begin:begin + count]  19.3 us
    slice x16, local copies, waits for them, and re-layouts, transpose_step(): jnp.roll(centre, 1, axis=2)  16.1 us
    ppermute x9, starting transfers between devices, with_halo(): lax.ppermute(head, axis, [((i + 1) % count, i) for i in range(ends)])  11.6 us
    slice x8, local copies, waits for them, and re-layouts, with_halo(): lax.slice_in_dim(cells, cells.shape[dim] - width, cells.shape[dim], axis=...  8.1 us
    unnamed x55, local copies, waits for them, and re-layouts  7.25 us
  transfers between devices with their start and end apart: 18, of which 0 were waited for; matrix products, arithmetic and copies ran while one was open for 16% of the time, Pallas kernels for 0%

commit v1 on v0

--- a/solution.py
+++ b/solution.py
@@ -5,6 +5,12 @@
 
 SUBSTEPS = 4
 HIGH = lax.Precision.HIGHEST
+
+
+def summed_here(block, axis):
+    shards = lax.all_gather(block, axis, axis=0, tiled=False)
+    summed = shards.sum(axis=0)
+    return summed
 
 
 def with_halo(cells, sides, width):
@@ -112,7 +118,7 @@
     )
 
     def month_total(local_grad):
-        return lax.psum(local_grad, "tile")
+        return summed_here(local_grad, "tile")
 
     total_two = month_total(grad_two)
     initial, sens_one, grad_one = month_adjoint(

time: 274 us -> 283 us (1.033)
  blocking collectives: 45.8 us -> 54.4 us
    all_gather x0 -> x2, blocking collectives: none -> 54.4 us  [summed_here(): shards = lax.all_gather(block, axis, axis=0, tiled=False)]
    psum x1 -> x0, blocking collectives: 45.8 us -> none  [month_total(): return lax.psum(local_grad, 'tile')]
  transfers between devices with their start and end apart: 18 -> 18, of which waited for: 0 -> 0; matrix products, arithmetic and copies ran while one was open for 16% -> 15% of each run, Pallas kernels for 0% -> 0%
where the time goes in v1:
time: 283 us; the launch traced here: 282 us
  starting transfers between devices  97.7 us (35%)
  local copies, waits for them, and re-layouts  59.1 us (21%)
  blocking collectives  54.4 us (19%)
  other arithmetic  50.8 us (18%)
  matrix products  17.2 us (6%)
    ppermute x9, starting transfers between devices, with_halo(): lax.ppermute(tail, axis, [(i, (i + 1) % count) for i in range(ends)])  86.1 us
    all_gather x2, blocking collectives, summed_here(): shards = lax.all_gather(block, axis, axis=0, tiled=False)  54.4 us
    add x8, other arithmetic, transpose_step(): keep * centre + rate_n * padded[:, :-2] + rate_s * padded[:, 2:]  47.6 us
    slice x40, local copies, waits for them, and re-layouts, transpose_step(): r[begin:begin + count]  19.2 us
    slice x16, local copies, waits for them, and re-layouts, transpose_step(): jnp.roll(centre, 1, axis=2)  16.1 us
    ppermute x9, starting transfers between devices, with_halo(): lax.ppermute(head, axis, [((i + 1) % count, i) for i in range(ends)])  11.6 us
    slice x8, local copies, waits for them, and re-layouts, with_halo(): lax.slice_in_dim(cells, cells.shape[dim] - width, cells.shape[dim], axis=...  8.1 us
    unnamed x55, local copies, waits for them, and re-layouts  7.24 us
  transfers between devices with their start and end apart: 18, of which 0 were waited for; matrix products, arithmetic and copies ran while one was open for 15% of the time, Pallas kernels for 0%

profile of v1, /device:TPU:0, one launch (start us, length us, event | category | flops | bytes accessed | tf_op | source)
XLA Modules:
  0.0 282.0 jit_solution(13286658116738015424)
XLA Ops:
  1.4 2.4 collective-permute-start.4
  3.8 1.3 collective-permute-start.5
  7.3 0.7 fusion.46
  8.0 0.7 fusion.47
  8.8 2.4 fusion.15
  11.2 2.4 fusion.13
  13.8 0.7 subtract_subtract_fusion
  14.5 94.6 %while.20 = (s32[]{:T(128)}, f32[160,2,1024]{2,1,0:T(2,128)S(1)}, f32[4,1024]{1,0:T(4,128)}, f32[4,1024]{1,0:T(4,128)}, f32[4,1024]{1,0:T(4,128)}, /*index=5*/f32[4,1024]{1,0:T(4,128)}, f32[4,1024]{1,0:T(4,128)}, s32[]{:T(128)}) while((s32[]{:T(128)}, f32[160,2,1024]{2,1,0:T(2,128)S(1)}, f32[4,1024]{1,0:T(4,128)}, f32[4,1024]{1,0:T(4,128)}, ...), condition=%wide.region_1.2_spmd, body=%wide.region_0.1_spmd.sunk | while | flops 4259842 | bytes 22864288 | solution.py:67
  15.1 1.0 fusion.71
  16.1 1.3 collective-permute-start
  17.4 6.6 %collective-permute-start.1 = (f32[160,1,1024]{2,1,0:T(1,128)S(1)}, f32[160,1,1024]{2,1,0:T(1,128)}, u32[]{:S(2)}, u32[]{:S(2)}) collective-permute-start(f32[160,1,1024]{2,1,0:T(1,128)S(1)} %get-tuple-element.228), channel_id=1, source_target_pairs={{0,1},{1,2},{2,3},{3,4},{4,5},{5,6},{6,7},{7,8},{8,9},{9,10},{10,1... | collective-permute-start | bytes 1966088 | tf_op jit(solution)/shard_map/while/body/eval_jaxpr/ppermute | solution.py:24
  26.7 1.8 fusion.73
  28.6 5.9 %fusion.74 = f32[160,2,1024]{2,1,0:T(2,128)S(1)} fusion(f32[160,1,1024]{2,1,0:T(1,128)S(1)} %collective-permute-done, f32[160,2,1024]{2,1,0:T(2,128)S(1)} %copy.37, f32[160,1,1024]{2,1,0:T(1,128)} %collective-permute-done.1, f32[160,2,1]{2,1,0:T(2,128)S(1)} %get-tuple-element.229, f32[160,2,1023]{2,1,0:T(2,128)S(1)} %get-tuple-element.230, ...), kind=kLoop, calls=%fused_computation.4.clone.1 | loop fusion | flops 4259840 | bytes 6594560 | tf_op jit(solution)/shard_map/while/body/eval_jaxpr/add | solution.py:52
  35.1 1.0 fusion.71
  36.1 1.3 collective-permute-start
  37.4 13.3 %collective-permute-start.1 = (f32[160,1,1024]{2,1,0:T(1,128)S(1)}, f32[160,1,1024]{2,1,0:T(1,128)}, u32[]{:S(2)}, u32[]{:S(2)}) collective-permute-start(f32[160,1,1024]{2,1,0:T(1,128)S(1)} %get-tuple-element.228), channel_id=1, source_target_pairs={{0,1},{1,2},{2,3},{3,4},{4,5},{5,6},{6,7},{7,8},{8,9},{9,10},{10,1... | collective-permute-start | bytes 1966088 | tf_op jit(solution)/shard_map/while/body/eval_jaxpr/ppermute | solution.py:24
  53.4 1.8 fusion.73
  55.2 5.9 %fusion.74 = f32[160,2,1024]{2,1,0:T(2,128)S(1)} fusion(f32[160,1,1024]{2,1,0:T(1,128)S(1)} %collective-permute-done, f32[160,2,1024]{2,1,0:T(2,128)S(1)} %copy.37, f32[160,1,1024]{2,1,0:T(1,128)} %collective-permute-done.1, f32[160,2,1]{2,1,0:T(2,128)S(1)} %get-tuple-element.229, f32[160,2,1023]{2,1,0:T(2,128)S(1)} %get-tuple-element.230, ...), kind=kLoop, calls=%fused_computation.4.clone.1 | loop fusion | flops 4259840 | bytes 6594560 | tf_op jit(solution)/shard_map/while/body/eval_jaxpr/add | solution.py:52
  61.7 1.0 fusion.71
  62.7 1.3 collective-permute-start
  64.0 9.1 %collective-permute-start.1 = (f32[160,1,1024]{2,1,0:T(1,128)S(1)}, f32[160,1,1024]{2,1,0:T(1,128)}, u32[]{:S(2)}, u32[]{:S(2)}) collective-permute-start(f32[160,1,1024]{2,1,0:T(1,128)S(1)} %get-tuple-element.228), channel_id=1, source_target_pairs={{0,1},{1,2},{2,3},{3,4},{4,5},{5,6},{6,7},{7,8},{8,9},{9,10},{10,1... | collective-permute-start | bytes 1966088 | tf_op jit(solution)/shard_map/while/body/eval_jaxpr/ppermute | solution.py:24
  75.9 1.8 fusion.73
  77.7 5.9 %fusion.74 = f32[160,2,1024]{2,1,0:T(2,128)S(1)} fusion(f32[160,1,1024]{2,1,0:T(1,128)S(1)} %collective-permute-done, f32[160,2,1024]{2,1,0:T(2,128)S(1)} %copy.37, f32[160,1,1024]{2,1,0:T(1,128)} %collective-permute-done.1, f32[160,2,1]{2,1,0:T(2,128)S(1)} %get-tuple-element.229, f32[160,2,1023]{2,1,0:T(2,128)S(1)} %get-tuple-element.230, ...), kind=kLoop, calls=%fused_computation.4.clone.1 | loop fusion | flops 4259840 | bytes 6594560 | tf_op jit(solution)/shard_map/while/body/eval_jaxpr/add | solution.py:52
  84.2 1.0 fusion.71
  85.2 1.3 collective-permute-start
  86.5 12.1 %collective-permute-start.1 = (f32[160,1,1024]{2,1,0:T(1,128)S(1)}, f32[160,1,1024]{2,1,0:T(1,128)}, u32[]{:S(2)}, u32[]{:S(2)}) collective-permute-start(f32[160,1,1024]{2,1,0:T(1,128)S(1)} %get-tuple-element.228), channel_id=1, source_target_pairs={{0,1},{1,2},{2,3},{3,4},{4,5},{5,6},{6,7},{7,8},{8,9},{9,10},{10,1... | collective-permute-start | bytes 1966088 | tf_op jit(solution)/shard_map/while/body/eval_jaxpr/ppermute | solution.py:24
  101.4 1.8 fusion.73
  103.2 5.9 %fusion.74 = f32[160,2,1024]{2,1,0:T(2,128)S(1)} fusion(f32[160,1,1024]{2,1,0:T(1,128)S(1)} %collective-permute-done, f32[160,2,1024]{2,1,0:T(2,128)S(1)} %copy.37, f32[160,1,1024]{2,1,0:T(1,128)} %collective-permute-done.1, f32[160,2,1]{2,1,0:T(2,128)S(1)} %get-tuple-element.229, f32[160,2,1023]{2,1,0:T(2,128)S(1)} %get-tuple-element.230, ...), kind=kLoop, calls=%fused_computation.4.clone.1 | loop fusion | flops 4259840 | bytes 6594560 | tf_op jit(solution)/shard_map/while/body/eval_jaxpr/add | solution.py:52
  110.7 0.8 copy-done.5
  111.9 1.8 fusion.30
  113.7 1.5 multiply_divide_fusion
  115.9 1.4 convolution_add_fusion.2
  117.2 1.1 reshape.61
  118.3 96.1 %while.21 = (s32[]{:T(128)}, f32[160,2,1024]{2,1,0:T(2,128)S(1)}, f32[4,1024]{1,0:T(4,128)}, f32[4,1024]{1,0:T(4,128)}, f32[4,1024]{1,0:T(4,128)}, /*index=5*/f32[4,1024]{1,0:T(4,128)}, f32[4,1024]{1,0:T(4,128)}, s32[]{:T(128)}) while((s32[]{:T(128)}, f32[160,2,1024]{2,1,0:T(2,128)S(1)}, f32[4,1024]{1,0:T(4,128)}, f32[4,1024]{1,0:T(4,128)}, ...), condition=%wide.region_3.4_spmd, body=%wide.region_2.3_spmd.sunk | while | flops 4259842 | bytes 22864288 | solution.py:67
  119.1 1.0 fusion.75
  120.1 1.3 collective-permute-start.2
  121.4 9.1 %collective-permute-start.3 = (f32[160,1,1024]{2,1,0:T(1,128)S(1)}, f32[160,1,1024]{2,1,0:T(1,128)}, u32[]{:S(2)}, u32[]{:S(2)}) collective-permute-start(f32[160,1,1024]{2,1,0:T(1,128)S(1)} %get-tuple-element.241), channel_id=1, source_target_pairs={{0,1},{1,2},{2,3},{3,4},{4,5},{5,6},{6,7},{7,8},{8,9},{9,10},{10,1... | collective-permute-start | bytes 1966088 | tf_op jit(solution)/shard_map/while/body/eval_jaxpr/ppermute | solution.py:24
  133.2 1.8 fusion.77
  135.1 5.9 %fusion.78 = f32[160,2,1024]{2,1,0:T(2,128)S(1)} fusion(f32[160,1,1024]{2,1,0:T(1,128)S(1)} %collective-permute-done.2, f32[160,2,1024]{2,1,0:T(2,128)S(1)} %copy.38, f32[160,1,1024]{2,1,0:T(1,128)} %collective-permute-done.3, f32[160,2,1]{2,1,0:T(2,128)S(1)} %get-tuple-element.242, f32[160,2,1023]{2,1,0:T(2,128)S(1)} %get-tuple-element.243, ...), kind=kLoop, calls=%fused_computation.14.clone.1 | loop fusion | flops 4259840 | bytes 6594560 | tf_op jit(solution)/shard_map/while/body/eval_jaxpr/add | solution.py:52
  141.5 1.0 fusion.75
  142.6 1.3 collective-permute-start.2
  143.9 12.2 %collective-permute-start.3 = (f32[160,1,1024]{2,1,0:T(1,128)S(1)}, f32[160,1,1024]{2,1,0:T(1,128)}, u32[]{:S(2)}, u32[]{:S(2)}) collective-permute-start(f32[160,1,1024]{2,1,0:T(1,128)S(1)} %get-tuple-element.241), channel_id=1, source_target_pairs={{0,1},{1,2},{2,3},{3,4},{4,5},{5,6},{6,7},{7,8},{8,9},{9,10},{10,1... | collective-permute-start | bytes 1966088 | tf_op jit(solution)/shard_map/while/body/eval_jaxpr/ppermute | solution.py:24
  158.7 1.8 fusion.77
  160.6 5.9 %fusion.78 = f32[160,2,1024]{2,1,0:T(2,128)S(1)} fusion(f32[160,1,1024]{2,1,0:T(1,128)S(1)} %collective-permute-done.2, f32[160,2,1024]{2,1,0:T(2,128)S(1)} %copy.38, f32[160,1,1024]{2,1,0:T(1,128)} %collective-permute-done.3, f32[160,2,1]{2,1,0:T(2,128)S(1)} %get-tuple-element.242, f32[160,2,1023]{2,1,0:T(2,128)S(1)} %get-tuple-element.243, ...), kind=kLoop, calls=%fused_computation.14.clone.1 | loop fusion | flops 4259840 | bytes 6594560 | tf_op jit(solution)/shard_map/while/body/eval_jaxpr/add | solution.py:52
  167.1 1.0 fusion.75
  168.1 1.3 collective-permute-start.2
  169.4 9.2 %collective-permute-start.3 = (f32[160,1,1024]{2,1,0:T(1,128)S(1)}, f32[160,1,1024]{2,1,0:T(1,128)}, u32[]{:S(2)}, u32[]{:S(2)}) collective-permute-start(f32[160,1,1024]{2,1,0:T(1,128)S(1)} %get-tuple-element.241), channel_id=1, source_target_pairs={{0,1},{1,2},{2,3},{3,4},{4,5},{5,6},{6,7},{7,8},{8,9},{9,10},{10,1... | collective-permute-start | bytes 1966088 | tf_op jit(solution)/shard_map/while/body/eval_jaxpr/ppermute | solution.py:24
  181.3 1.8 fusion.77
  183.1 5.9 %fusion.78 = f32[160,2,1024]{2,1,0:T(2,128)S(1)} fusion(f32[160,1,1024]{2,1,0:T(1,128)S(1)} %collective-permute-done.2, f32[160,2,1024]{2,1,0:T(2,128)S(1)} %copy.38, f32[160,1,1024]{2,1,0:T(1,128)} %collective-permute-done.3, f32[160,2,1]{2,1,0:T(2,128)S(1)} %get-tuple-element.242, f32[160,2,1023]{2,1,0:T(2,128)S(1)} %get-tuple-element.243, ...), kind=kLoop, calls=%fused_computation.14.clone.1 | loop fusion | flops 4259840 | bytes 6594560 | tf_op jit(solution)/shard_map/while/body/eval_jaxpr/add | solution.py:52
  189.6 1.0 fusion.75
  190.6 1.3 collective-permute-start.2
  191.9 12.0 %collective-permute-start.3 = (f32[160,1,1024]{2,1,0:T(1,128)S(1)}, f32[160,1,1024]{2,1,0:T(1,128)}, u32[]{:S(2)}, u32[]{:S(2)}) collective-permute-start(f32[160,1,1024]{2,1,0:T(1,128)S(1)} %get-tuple-element.241), channel_id=1, source_target_pairs={{0,1},{1,2},{2,3},{3,4},{4,5},{5,6},{6,7},{7,8},{8,9},{9,10},{10,1... | collective-permute-start | bytes 1966088 | tf_op jit(solution)/shard_map/while/body/eval_jaxpr/ppermute | solution.py:24
  206.7 1.8 fusion.77
  208.5 5.9 %fusion.78 = f32[160,2,1024]{2,1,0:T(2,128)S(1)} fusion(f32[160,1,1024]{2,1,0:T(1,128)S(1)} %collective-permute-done.2, f32[160,2,1024]{2,1,0:T(2,128)S(1)} %copy.38, f32[160,1,1024]{2,1,0:T(1,128)} %collective-permute-done.3, f32[160,2,1]{2,1,0:T(2,128)S(1)} %get-tuple-element.242, f32[160,2,1023]{2,1,0:T(2,128)S(1)} %get-tuple-element.243, ...), kind=kLoop, calls=%fused_computation.14.clone.1 | loop fusion | flops 4259840 | bytes 6594560 | tf_op jit(solution)/shard_map/while/body/eval_jaxpr/add | solution.py:52
  216.0 0.8 copy-done.3
  217.3 1.2 fusion.31
  218.5 0.8 multiply_divide_fusion.1
  219.8 1.2 fusion.16
  221.2 36.8 %all-gather.3 = f32[16,16,6]{1,2,0:T(8,128)S(1)} all-gather(f32[1,16,6]{1,2,0:T(8,128)S(1)} %convolution_bitcast_fusion.2), channel_id=3, replica_groups=mesh['ens'=2,'tile'=16] {'tile'}, dimensions={0}, use_global_device_ids=true | all-gather | bytes 6528 | tf_op jit(solution)/shard_map/all_gather | solution.py:11
  258.0 1.4 convolution_add_fusion
  259.4 1.2 fusion.17
  260.8 17.6 %all-gather.2 = f32[16,16,6]{1,2,0:T(8,128)S(1)} all-gather(f32[1,16,6]{1,2,0:T(8,128)S(1)} %convolution_bitcast_fusion.3), channel_id=2, replica_groups=mesh['ens'=2,'tile'=16] {'tile'}, dimensions={0}, use_global_device_ids=true | all-gather | bytes 6528 | tf_op jit(solution)/shard_map/all_gather | solution.py:11
  278.6 2.2 reshape.64
  281.3 0.7 pad_maximum_fusion.6
  (290 shorter events, 34.2 us)
Async XLA Ops:
  0.6 6.3 %copy-start = (f32[16,6]{0,1:T(8,128)S(1)}, f32[16,6]{0,1:T(8,128)}, u32[]{:S(2)}) copy-start(f32[16,6]{0,1:T(8,128)} %param.18) | copy-start | bytes 1156
  0.7 4.4 %copy-start.9 = (f32[160,2,1024]{2,1,0:T(2,128)S(1)}, f32[160,2,1024]{2,1,0:T(2,128)}, u32[]{:S(2)}) copy-start(f32[160,2,1024]{2,1,0:T(2,128)} %param.16) | copy-start | bytes 3932164
  1.4 12.3 %collective-permute-start.4 = (f32[3,2,1024]{2,1,0:T(2,128)S(1)}, f32[3,2,1024]{2,1,0:T(2,128)S(1)}, u32[]{:S(2)}, u32[]{:S(2)}) collective-permute-start(f32[3,2,1024]{2,1,0:T(2,128)S(1)} %pad_maximum_fusion.7), channel_id=1, source_target_pairs={{0,1},{1,2},{2,3},{3,4},{4,5},{5,6},{6,7},{7,8},{8,9},{9,10},{10,1... | collective-permute-start | bytes 73736 | tf_op jit(solution)/shard_map/ppermute | solution.py:24
  3.8 9.9 %collective-permute-start.5 = (f32[3,2,1024]{2,1,0:T(2,128)S(1)}, f32[3,2,1024]{2,1,0:T(2,128)S(1)}, u32[]{:S(2)}, u32[]{:S(2)}) collective-permute-start(f32[3,2,1024]{2,1,0:T(2,128)S(1)} %pad_maximum_fusion.7), channel_id=1, source_target_pairs={{1,0},{2,1},{3,2},{4,3},{5,4},{6,5},{7,6},{8,7},{9,8},{10,9},{11,1... | collective-permute-start | bytes 73736 | tf_op jit(solution)/shard_map/ppermute | solution.py:26
  7.3 3.9 %copy-start.19 = (f32[160,6]{0,1:T(8,128)}, f32[160,6]{0,1:T(8,128)S(1)}, u32[]{:S(2)}) copy-start(f32[160,6]{0,1:T(8,128)S(1)} %fusion.26) | copy-start | bytes 11524
  8.8 5.7 %copy-start.1 = (f32[160,2,1024]{2,1,0:T(2,128)S(1)}, f32[160,2,1024]{2,1,0:T(2,128)}, u32[]{:S(2)}) copy-start(f32[160,2,1024]{2,1,0:T(2,128)} %param.14) | copy-start | bytes 3932164
  15.0 9.0 %copy-start.32 = (f32[4,1024]{1,0:T(4,128)S(1)}, f32[4,1024]{1,0:T(4,128)}, u32[]{:S(2)}) copy-start(f32[4,1024]{1,0:T(4,128)} %get-tuple-element.268) | copy-start | bytes 49156 | tf_op jit(solution)/shard_map/while
  15.0 9.0 %copy-start.30 = (f32[4,1024]{1,0:T(4,128)S(1)}, f32[4,1024]{1,0:T(4,128)}, u32[]{:S(2)}) copy-start(f32[4,1024]{1,0:T(4,128)} %get-tuple-element.267) | copy-start | bytes 49156 | tf_op jit(solution)/shard_map/while
  15.0 9.6 %copy-start.28 = (f32[4,1024]{1,0:T(4,128)S(1)}, f32[4,1024]{1,0:T(4,128)}, u32[]{:S(2)}) copy-start(f32[4,1024]{1,0:T(4,128)} %get-tuple-element.266) | copy-start | bytes 49156 | tf_op jit(solution)/shard_map/while
  15.0 10.2 %copy-start.26 = (f32[4,1024]{1,0:T(4,128)S(1)}, f32[4,1024]{1,0:T(4,128)}, u32[]{:S(2)}) copy-start(f32[4,1024]{1,0:T(4,128)} %get-tuple-element.265) | copy-start | bytes 49156 | tf_op jit(solution)/shard_map/while
  15.0 10.8 %copy-start.24 = (f32[4,1024]{1,0:T(4,128)S(1)}, f32[4,1024]{1,0:T(4,128)}, u32[]{:S(2)}) copy-start(f32[4,1024]{1,0:T(4,128)} %get-tuple-element.264) | copy-start | bytes 49156 | tf_op jit(solution)/shard_map/while
  16.1 12.4 %collective-permute-start = (f32[160,1,1024]{2,1,0:T(1,128)S(1)}, f32[160,1,1024]{2,1,0:T(1,128)S(1)}, u32[]{:S(2)}, u32[]{:S(2)}) collective-permute-start(f32[160,1,1024]{2,1,0:T(1,128)S(1)} %get-tuple-element.227), channel_id=1, source_target_pairs={{1,0},{2,1},{3,2},{4,3},{5,4},{6,5},{7,6},{8,7},{9,8},{10,9},{11,1... | collective-permute-start | bytes 1966088 | tf_op jit(solution)/shard_map/while/body/eval_jaxpr/ppermute | solution.py:26
  17.4 11.2 %collective-permute-start.1 = (f32[160,1,1024]{2,1,0:T(1,128)S(1)}, f32[160,1,1024]{2,1,0:T(1,128)}, u32[]{:S(2)}, u32[]{:S(2)}) collective-permute-start(f32[160,1,1024]{2,1,0:T(1,128)S(1)} %get-tuple-element.228), channel_id=1, source_target_pairs={{0,1},{1,2},{2,3},{3,4},{4,5},{5,6},{6,7},{7,8},{8,9},{9,10},{10,1... | collective-permute-start | bytes 1966088 | tf_op jit(solution)/shard_map/while/body/eval_jaxpr/ppermute | solution.py:24
  26.7 1.9 copy-start.11
  35.0 15.7 %copy-start.32 = (f32[4,1024]{1,0:T(4,128)S(1)}, f32[4,1024]{1,0:T(4,128)}, u32[]{:S(2)}) copy-start(f32[4,1024]{1,0:T(4,128)} %get-tuple-element.268) | copy-start | bytes 49156 | tf_op jit(solution)/shard_map/while
  35.0 15.7 %copy-start.30 = (f32[4,1024]{1,0:T(4,128)S(1)}, f32[4,1024]{1,0:T(4,128)}, u32[]{:S(2)}) copy-start(f32[4,1024]{1,0:T(4,128)} %get-tuple-element.267) | copy-start | bytes 49156 | tf_op jit(solution)/shard_map/while
  35.0 16.3 %copy-start.28 = (f32[4,1024]{1,0:T(4,128)S(1)}, f32[4,1024]{1,0:T(4,128)}, u32[]{:S(2)}) copy-start(f32[4,1024]{1,0:T(4,128)} %get-tuple-element.266) | copy-start | bytes 49156 | tf_op jit(solution)/shard_map/while
  35.0 16.9 %copy-start.26 = (f32[4,1024]{1,0:T(4,128)S(1)}, f32[4,1024]{1,0:T(4,128)}, u32[]{:S(2)}) copy-start(f32[4,1024]{1,0:T(4,128)} %get-tuple-element.265) | copy-start | bytes 49156 | tf_op jit(solution)/shard_map/while
  35.0 17.5 %copy-start.24 = (f32[4,1024]{1,0:T(4,128)S(1)}, f32[4,1024]{1,0:T(4,128)}, u32[]{:S(2)}) copy-start(f32[4,1024]{1,0:T(4,128)} %get-tuple-element.264) | copy-start | bytes 49156 | tf_op jit(solution)/shard_map/while
  36.1 19.1 %collective-permute-start = (f32[160,1,1024]{2,1,0:T(1,128)S(1)}, f32[160,1,1024]{2,1,0:T(1,128)S(1)}, u32[]{:S(2)}, u32[]{:S(2)}) collective-permute-start(f32[160,1,1024]{2,1,0:T(1,128)S(1)} %get-tuple-element.227), channel_id=1, source_target_pairs={{1,0},{2,1},{3,2},{4,3},{5,4},{6,5},{7,6},{8,7},{9,8},{10,9},{11,1... | collective-permute-start | bytes 1966088 | tf_op jit(solution)/shard_map/while/body/eval_jaxpr/ppermute | solution.py:26
  37.4 17.8 %collective-permute-start.1 = (f32[160,1,1024]{2,1,0:T(1,128)S(1)}, f32[160,1,1024]{2,1,0:T(1,128)}, u32[]{:S(2)}, u32[]{:S(2)}) collective-permute-start(f32[160,1,1024]{2,1,0:T(1,128)S(1)} %get-tuple-element.228), channel_id=1, source_target_pairs={{0,1},{1,2},{2,3},{3,4},{4,5},{5,6},{6,7},{7,8},{8,9},{9,10},{10,1... | collective-permute-start | bytes 1966088 | tf_op jit(solution)/shard_map/while/body/eval_jaxpr/ppermute | solution.py:24
  61.7 11.5 %copy-start.32 = (f32[4,1024]{1,0:T(4,128)S(1)}, f32[4,1024]{1,0:T(4,128)}, u32[]{:S(2)}) copy-start(f32[4,1024]{1,0:T(4,128)} %get-tuple-element.268) | copy-start | bytes 49156 | tf_op jit(solution)/shard_map/while
  61.7 11.5 %copy-start.30 = (f32[4,1024]{1,0:T(4,128)S(1)}, f32[4,1024]{1,0:T(4,128)}, u32[]{:S(2)}) copy-start(f32[4,1024]{1,0:T(4,128)} %get-tuple-element.267) | copy-start | bytes 49156 | tf_op jit(solution)/shard_map/while
  61.7 12.1 %copy-start.28 = (f32[4,1024]{1,0:T(4,128)S(1)}, f32[4,1024]{1,0:T(4,128)}, u32[]{:S(2)}) copy-start(f32[4,1024]{1,0:T(4,128)} %get-tuple-element.266) | copy-start | bytes 49156 | tf_op jit(solution)/shard_map/while
  61.7 12.7 %copy-start.26 = (f32[4,1024]{1,0:T(4,128)S(1)}, f32[4,1024]{1,0:T(4,128)}, u32[]{:S(2)}) copy-start(f32[4,1024]{1,0:T(4,128)} %get-tuple-element.265) | copy-start | bytes 49156 | tf_op jit(solution)/shard_map/while
  61.7 13.3 %copy-start.24 = (f32[4,1024]{1,0:T(4,128)S(1)}, f32[4,1024]{1,0:T(4,128)}, u32[]{:S(2)}) copy-start(f32[4,1024]{1,0:T(4,128)} %get-tuple-element.264) | copy-start | bytes 49156 | tf_op jit(solution)/shard_map/while
  62.7 14.9 %collective-permute-start = (f32[160,1,1024]{2,1,0:T(1,128)S(1)}, f32[160,1,1024]{2,1,0:T(1,128)S(1)}, u32[]{:S(2)}, u32[]{:S(2)}) collective-permute-start(f32[160,1,1024]{2,1,0:T(1,128)S(1)} %get-tuple-element.227), channel_id=1, source_target_pairs={{1,0},{2,1},{3,2},{4,3},{5,4},{6,5},{7,6},{8,7},{9,8},{10,9},{11,1... | collective-permute-start | bytes 1966088 | tf_op jit(solution)/shard_map/while/body/eval_jaxpr/ppermute | solution.py:26
  64.0 13.6 %collective-permute-start.1 = (f32[160,1,1024]{2,1,0:T(1,128)S(1)}, f32[160,1,1024]{2,1,0:T(1,128)}, u32[]{:S(2)}, u32[]{:S(2)}) collective-permute-start(f32[160,1,1024]{2,1,0:T(1,128)S(1)} %get-tuple-element.228), channel_id=1, source_target_pairs={{0,1},{1,2},{2,3},{3,4},{4,5},{5,6},{6,7},{7,8},{8,9},{9,10},{10,1... | collective-permute-start | bytes 1966088 | tf_op jit(solution)/shard_map/while/body/eval_jaxpr/ppermute | solution.py:24
  84.1 14.5 %copy-start.32 = (f32[4,1024]{1,0:T(4,128)S(1)}, f32[4,1024]{1,0:T(4,128)}, u32[]{:S(2)}) copy-start(f32[4,1024]{1,0:T(4,128)} %get-tuple-element.268) | copy-start | bytes 49156 | tf_op jit(solution)/shard_map/while
  84.1 14.5 %copy-start.30 = (f32[4,1024]{1,0:T(4,128)S(1)}, f32[4,1024]{1,0:T(4,128)}, u32[]{:S(2)}) copy-start(f32[4,1024]{1,0:T(4,128)} %get-tuple-element.267) | copy-start | bytes 49156 | tf_op jit(solution)/shard_map/while
  84.2 15.1 %copy-start.28 = (f32[4,1024]{1,0:T(4,128)S(1)}, f32[4,1024]{1,0:T(4,128)}, u32[]{:S(2)}) copy-start(f32[4,1024]{1,0:T(4,128)} %get-tuple-element.266) | copy-start | bytes 49156 | tf_op jit(solution)/shard_map/while
  84.2 15.7 %copy-start.26 = (f32[4,1024]{1,0:T(4,128)S(1)}, f32[4,1024]{1,0:T(4,128)}, u32[]{:S(2)}) copy-start(f32[4,1024]{1,0:T(4,128)} %get-tuple-element.265) | copy-start | bytes 49156 | tf_op jit(solution)/shard_map/while
  84.2 16.3 %copy-start.24 = (f32[4,1024]{1,0:T(4,128)S(1)}, f32[4,1024]{1,0:T(4,128)}, u32[]{:S(2)}) copy-start(f32[4,1024]{1,0:T(4,128)} %get-tuple-element.264) | copy-start | bytes 49156 | tf_op jit(solution)/shard_map/while
  85.2 17.9 %collective-permute-start = (f32[160,1,1024]{2,1,0:T(1,128)S(1)}, f32[160,1,1024]{2,1,0:T(1,128)S(1)}, u32[]{:S(2)}, u32[]{:S(2)}) collective-permute-start(f32[160,1,1024]{2,1,0:T(1,128)S(1)} %get-tuple-element.227), channel_id=1, source_target_pairs={{1,0},{2,1},{3,2},{4,3},{5,4},{6,5},{7,6},{8,7},{9,8},{10,9},{11,1... | collective-permute-start | bytes 1966088 | tf_op jit(solution)/shard_map/while/body/eval_jaxpr/ppermute | solution.py:26
  86.5 16.7 %collective-permute-start.1 = (f32[160,1,1024]{2,1,0:T(1,128)S(1)}, f32[160,1,1024]{2,1,0:T(1,128)}, u32[]{:S(2)}, u32[]{:S(2)}) collective-permute-start(f32[160,1,1024]{2,1,0:T(1,128)S(1)} %get-tuple-element.228), channel_id=1, source_target_pairs={{0,1},{1,2},{2,3},{3,4},{4,5},{5,6},{6,7},{7,8},{8,9},{9,10},{10,1... | collective-permute-start | bytes 1966088 | tf_op jit(solution)/shard_map/while/body/eval_jaxpr/ppermute | solution.py:24
  119.0 11.5 %copy-start.33 = (f32[4,1024]{1,0:T(4,128)S(1)}, f32[4,1024]{1,0:T(4,128)}, u32[]{:S(2)}) copy-start(f32[4,1024]{1,0:T(4,128)} %get-tuple-element.292) | copy-start | bytes 49156 | tf_op jit(solution)/shard_map/while
  119.0 11.5 %copy-start.31 = (f32[4,1024]{1,0:T(4,128)S(1)}, f32[4,1024]{1,0:T(4,128)}, u32[]{:S(2)}) copy-start(f32[4,1024]{1,0:T(4,128)} %get-tuple-element.291) | copy-start | bytes 49156 | tf_op jit(solution)/shard_map/while
  119.1 12.1 %copy-start.29 = (f32[4,1024]{1,0:T(4,128)S(1)}, f32[4,1024]{1,0:T(4,128)}, u32[]{:S(2)}) copy-start(f32[4,1024]{1,0:T(4,128)} %get-tuple-element.290) | copy-start | bytes 49156 | tf_op jit(solution)/shard_map/while
  119.1 12.7 %copy-start.27 = (f32[4,1024]{1,0:T(4,128)S(1)}, f32[4,1024]{1,0:T(4,128)}, u32[]{:S(2)}) copy-start(f32[4,1024]{1,0:T(4,128)} %get-tuple-element.289) | copy-start | bytes 49156 | tf_op jit(solution)/shard_map/while
  119.1 13.3 %copy-start.25 = (f32[4,1024]{1,0:T(4,128)S(1)}, f32[4,1024]{1,0:T(4,128)}, u32[]{:S(2)}) copy-start(f32[4,1024]{1,0:T(4,128)} %get-tuple-element.288) | copy-start | bytes 49156 | tf_op jit(solution)/shard_map/while
  120.1 14.9 %collective-permute-start.2 = (f32[160,1,1024]{2,1,0:T(1,128)S(1)}, f32[160,1,1024]{2,1,0:T(1,128)S(1)}, u32[]{:S(2)}, u32[]{:S(2)}) collective-permute-start(f32[160,1,1024]{2,1,0:T(1,128)S(1)} %get-tuple-element.240), channel_id=1, source_target_pairs={{1,0},{2,1},{3,2},{4,3},{5,4},{6,5},{7,6},{8,7},{9,8},{10,9},{11,1... | collective-permute-start | bytes 1966088 | tf_op jit(solution)/shard_map/while/body/eval_jaxpr/ppermute | solution.py:26
  121.4 13.6 %collective-permute-start.3 = (f32[160,1,1024]{2,1,0:T(1,128)S(1)}, f32[160,1,1024]{2,1,0:T(1,128)}, u32[]{:S(2)}, u32[]{:S(2)}) collective-permute-start(f32[160,1,1024]{2,1,0:T(1,128)S(1)} %get-tuple-element.241), channel_id=1, source_target_pairs={{0,1},{1,2},{2,3},{3,4},{4,5},{5,6},{6,7},{7,8},{8,9},{9,10},{10,1... | collective-permute-start | bytes 1966088 | tf_op jit(solution)/shard_map/while/body/eval_jaxpr/ppermute | solution.py:24
  141.5 14.5 %copy-start.33 = (f32[4,1024]{1,0:T(4,128)S(1)}, f32[4,1024]{1,0:T(4,128)}, u32[]{:S(2)}) copy-start(f32[4,1024]{1,0:T(4,128)} %get-tuple-element.292) | copy-start | bytes 49156 | tf_op jit(solution)/shard_map/while
  141.5 14.5 %copy-start.31 = (f32[4,1024]{1,0:T(4,128)S(1)}, f32[4,1024]{1,0:T(4,128)}, u32[]{:S(2)}) copy-start(f32[4,1024]{1,0:T(4,128)} %get-tuple-element.291) | copy-start | bytes 49156 | tf_op jit(solution)/shard_map/while
  141.5 15.1 %copy-start.29 = (f32[4,1024]{1,0:T(4,128)S(1)}, f32[4,1024]{1,0:T(4,128)}, u32[]{:S(2)}) copy-start(f32[4,1024]{1,0:T(4,128)} %get-tuple-element.290) | copy-start | bytes 49156 | tf_op jit(solution)/shard_map/while
  141.5 15.7 %copy-start.27 = (f32[4,1024]{1,0:T(4,128)S(1)}, f32[4,1024]{1,0:T(4,128)}, u32[]{:S(2)}) copy-start(f32[4,1024]{1,0:T(4,128)} %get-tuple-element.289) | copy-start | bytes 49156 | tf_op jit(solution)/shard_map/while
  141.5 16.3 %copy-start.25 = (f32[4,1024]{1,0:T(4,128)S(1)}, f32[4,1024]{1,0:T(4,128)}, u32[]{:S(2)}) copy-start(f32[4,1024]{1,0:T(4,128)} %get-tuple-element.288) | copy-start | bytes 49156 | tf_op jit(solution)/shard_map/while
  142.6 17.9 %collective-permute-start.2 = (f32[160,1,1024]{2,1,0:T(1,128)S(1)}, f32[160,1,1024]{2,1,0:T(1,128)S(1)}, u32[]{:S(2)}, u32[]{:S(2)}) collective-permute-start(f32[160,1,1024]{2,1,0:T(1,128)S(1)} %get-tuple-element.240), channel_id=1, source_target_pairs={{1,0},{2,1},{3,2},{4,3},{5,4},{6,5},{7,6},{8,7},{9,8},{10,9},{11,1... | collective-permute-start | bytes 1966088 | tf_op jit(solution)/shard_map/while/body/eval_jaxpr/ppermute | solution.py:26
  143.9 16.7 %collective-permute-start.3 = (f32[160,1,1024]{2,1,0:T(1,128)S(1)}, f32[160,1,1024]{2,1,0:T(1,128)}, u32[]{:S(2)}, u32[]{:S(2)}) collective-permute-start(f32[160,1,1024]{2,1,0:T(1,128)S(1)} %get-tuple-element.241), channel_id=1, source_target_pairs={{0,1},{1,2},{2,3},{3,4},{4,5},{5,6},{6,7},{7,8},{8,9},{9,10},{10,1... | collective-permute-start | bytes 1966088 | tf_op jit(solution)/shard_map/while/body/eval_jaxpr/ppermute | solution.py:24
  167.0 11.6 %copy-start.33 = (f32[4,1024]{1,0:T(4,128)S(1)}, f32[4,1024]{1,0:T(4,128)}, u32[]{:S(2)}) copy-start(f32[4,1024]{1,0:T(4,128)} %get-tuple-element.292) | copy-start | bytes 49156 | tf_op jit(solution)/shard_map/while
  167.0 11.6 %copy-start.31 = (f32[4,1024]{1,0:T(4,128)S(1)}, f32[4,1024]{1,0:T(4,128)}, u32[]{:S(2)}) copy-start(f32[4,1024]{1,0:T(4,128)} %get-tuple-element.291) | copy-start | bytes 49156 | tf_op jit(solution)/shard_map/while
  167.0 12.2 %copy-start.29 = (f32[4,1024]{1,0:T(4,128)S(1)}, f32[4,1024]{1,0:T(4,128)}, u32[]{:S(2)}) copy-start(f32[4,1024]{1,0:T(4,128)} %get-tuple-element.290) | copy-start | bytes 49156 | tf_op jit(solution)/shard_map/while
  167.0 12.8 %copy-start.27 = (f32[4,1024]{1,0:T(4,128)S(1)}, f32[4,1024]{1,0:T(4,128)}, u32[]{:S(2)}) copy-start(f32[4,1024]{1,0:T(4,128)} %get-tuple-element.289) | copy-start | bytes 49156 | tf_op jit(solution)/shard_map/while
  167.0 13.4 %copy-start.25 = (f32[4,1024]{1,0:T(4,128)S(1)}, f32[4,1024]{1,0:T(4,128)}, u32[]{:S(2)}) copy-start(f32[4,1024]{1,0:T(4,128)} %get-tuple-element.288) | copy-start | bytes 49156 | tf_op jit(solution)/shard_map/while
  168.1 15.0 %collective-permute-start.2 = (f32[160,1,1024]{2,1,0:T(1,128)S(1)}, f32[160,1,1024]{2,1,0:T(1,128)S(1)}, u32[]{:S(2)}, u32[]{:S(2)}) collective-permute-start(f32[160,1,1024]{2,1,0:T(1,128)S(1)} %get-tuple-element.240), channel_id=1, source_target_pairs={{1,0},{2,1},{3,2},{4,3},{5,4},{6,5},{7,6},{8,7},{9,8},{10,9},{11,1... | collective-permute-start | bytes 1966088 | tf_op jit(solution)/shard_map/while/body/eval_jaxpr/ppermute | solution.py:26
  169.4 13.7 %collective-permute-start.3 = (f32[160,1,1024]{2,1,0:T(1,128)S(1)}, f32[160,1,1024]{2,1,0:T(1,128)}, u32[]{:S(2)}, u32[]{:S(2)}) collective-permute-start(f32[160,1,1024]{2,1,0:T(1,128)S(1)} %get-tuple-element.241), channel_id=1, source_target_pairs={{0,1},{1,2},{2,3},{3,4},{4,5},{5,6},{6,7},{7,8},{8,9},{9,10},{10,1... | collective-permute-start | bytes 1966088 | tf_op jit(solution)/shard_map/while/body/eval_jaxpr/ppermute | solution.py:24
  189.6 14.4 %copy-start.33 = (f32[4,1024]{1,0:T(4,128)S(1)}, f32[4,1024]{1,0:T(4,128)}, u32[]{:S(2)}) copy-start(f32[4,1024]{1,0:T(4,128)} %get-tuple-element.292) | copy-start | bytes 49156 | tf_op jit(solution)/shard_map/while
  189.6 14.4 %copy-start.31 = (f32[4,1024]{1,0:T(4,128)S(1)}, f32[4,1024]{1,0:T(4,128)}, u32[]{:S(2)}) copy-start(f32[4,1024]{1,0:T(4,128)} %get-tuple-element.291) | copy-start | bytes 49156 | tf_op jit(solution)/shard_map/while
  189.6 15.0 %copy-start.29 = (f32[4,1024]{1,0:T(4,128)S(1)}, f32[4,1024]{1,0:T(4,128)}, u32[]{:S(2)}) copy-start(f32[4,1024]{1,0:T(4,128)} %get-tuple-element.290) | copy-start | bytes 49156 | tf_op jit(solution)/shard_map/while
  189.6 15.6 %copy-start.27 = (f32[4,1024]{1,0:T(4,128)S(1)}, f32[4,1024]{1,0:T(4,128)}, u32[]{:S(2)}) copy-start(f32[4,1024]{1,0:T(4,128)} %get-tuple-element.289) | copy-start | bytes 49156 | tf_op jit(solution)/shard_map/while
  189.6 16.2 %copy-start.25 = (f32[4,1024]{1,0:T(4,128)S(1)}, f32[4,1024]{1,0:T(4,128)}, u32[]{:S(2)}) copy-start(f32[4,1024]{1,0:T(4,128)} %get-tuple-element.288) | copy-start | bytes 49156 | tf_op jit(solution)/shard_map/while
  190.6 17.8 %collective-permute-start.2 = (f32[160,1,1024]{2,1,0:T(1,128)S(1)}, f32[160,1,1024]{2,1,0:T(1,128)S(1)}, u32[]{:S(2)}, u32[]{:S(2)}) collective-permute-start(f32[160,1,1024]{2,1,0:T(1,128)S(1)} %get-tuple-element.240), channel_id=1, source_target_pairs={{1,0},{2,1},{3,2},{4,3},{5,4},{6,5},{7,6},{8,7},{9,8},{10,9},{11,1... | collective-permute-start | bytes 1966088 | tf_op jit(solution)/shard_map/while/body/eval_jaxpr/ppermute | solution.py:26
  191.9 16.6 %collective-permute-start.3 = (f32[160,1,1024]{2,1,0:T(1,128)S(1)}, f32[160,1,1024]{2,1,0:T(1,128)}, u32[]{:S(2)}, u32[]{:S(2)}) collective-permute-start(f32[160,1,1024]{2,1,0:T(1,128)S(1)} %get-tuple-element.241), channel_id=1, source_target_pairs={{0,1},{1,2},{2,3},{3,4},{4,5},{5,6},{6,7},{7,8},{8,9},{9,10},{10,1... | collective-permute-start | bytes 1966088 | tf_op jit(solution)/shard_map/while/body/eval_jaxpr/ppermute | solution.py:24
  259.4 19.1 %copy-start.35 = (f32[6,2048]{1,0:T(8,128)S(1)}, f32[6,2048]{1,0:T(8,128)}, u32[]{:S(2)}) copy-start(f32[6,2048]{1,0:T(8,128)} %get-tuple-element.132) | copy-start | bytes 147460
  (50 other events, 80.6 us)
